TPU v7x, 32 devices: a whole 2x2x4 slice. The times are simulated.
32 devices in a mesh: tm: 8 (over y, x, core), mp: 4 (over z).
Axes of the slice: x: 2, y: 2, z: 4, core: 2. Of those that a mesh axis runs over, the one named last changes fastest.
Arguments:
- frames: bfloat16 [4096, 1024], P(('tm', 'mp')), may hold values from -6 to 6
- block_ids: int32 [4096], replicated, may hold values from 0 to 203, never falling along the last dimension, each value on 1 to 40 neighbouring positions
- valid_counts: int32 [8], replicated, may hold values from 1 to 512, as said below
- norm_attn: float32 [1024], replicated, may hold values from 0.25 to 1.75
- w_qkv: bfloat16 [1024, 3072], replicated, may hold values from -1 to 1
- w_attn_out: bfloat16 [1024, 1024], replicated, may hold values from -0.1875 to 0.1875
- norm_conv: float32 [1024], replicated, may hold values from 0.25 to 1.75
- w_point_in: bfloat16 [1024, 2048], replicated, may hold values from -0.1875 to 0.1875
- w_depth: bfloat16 [31, 1024], replicated, may hold values from -1 to 1
- w_point_out: bfloat16 [1024, 1024], replicated, may hold values from -0.1875 to 0.1875
- w_adapter: bfloat16 [1024, 8192], P('tm', 'mp'), may hold values from -1 to 1
- llm_gain: float32 [8192], replicated, may hold values from 0.25 to 1.75
- w_query: bfloat16 [8192, 8192], P('tm', 'mp'), may hold values from -1 to 1
- w_key: bfloat16 [8192, 1024], P('tm', 'mp'), may hold values from -1 to 1
- w_value: bfloat16 [8192, 1024], P('tm', 'mp'), may hold values from -0.0625 to 0.0625
Outputs:
- conf_out: bfloat16 [4096, 1024], P(('tm', 'mp'))
- attended: bfloat16 [1024, 8192], P('tm', 'mp')
Inputs may be any that keep to these rules, and one draw needn't show every extreme that they name: `block_ids`: block numbers never fall along the recording, and one block holds 1 to 40 frames. Every time shard but the last holds 512 real frames; the frames after the first valid_counts[t] of time shard t are padding.
All inputs are finite; a program needn't handle non-finite values.
Results may differ from a plain program's by a relative error of at most 0.014.
Values may be sent and summed in bfloat16 or wider, within the bound.
No kernel may reach another device: no remote copies, remote signals or barrier semaphores. Data moves between devices by JAX's collectives and lax.ppermute only.
A program may use at most 192 MiB of HBM per device.

v0:
```python
import math
import jax
import jax.numpy as jnp
from jax import lax
from jax.sharding import PartitionSpec as P

CH = 16
HDIM = 128
eps_conf = 1e-05
eps_llm = 1e-06
rope_base = 1000000.0
masked_score = -1e30


def passed_along(value, axis, by):
    length = lax.axis_size(axis)
    pairs = [(i, i + by) for i in range(length) if 0 <= i + by < length]
    return lax.ppermute(value, axis, pairs)


def shard_count(index, valid_counts, shard_len):
    shard = index // shard_len
    table = jnp.arange(valid_counts.shape[0], dtype=jnp.int32)
    hit = shard[:, None] == table[None, :]
    count = jnp.sum(jnp.where(hit, valid_counts[None, :], 0), axis=1)
    return (index - shard * shard_len, count)


def layer_norm(field, gain):
    center = field - jnp.mean(field, axis=-1, keepdims=True)
    spread = jnp.mean(center * center, axis=-1, keepdims=True)
    return center * lax.rsqrt(spread + eps_conf) * gain


def rotary(field, positions):
    half = field.shape[-1] // 2
    freq = rope_base ** (-(jnp.arange(half, dtype=jnp.float32) * 2.0) / field.shape[-1])
    angle = positions.astype(jnp.float32)[:, None] * freq[None, :]
    cosine = jnp.concatenate([jnp.cos(angle), jnp.cos(angle)], axis=-1)[:, None, :]
    sine = jnp.concatenate([jnp.sin(angle), jnp.sin(angle)], axis=-1)[:, None, :]
    turned = jnp.concatenate([-field[..., half:], field[..., :half]], axis=-1)
    return field * cosine + turned * sine


def on_device(
    frames,
    block_ids,
    valid_counts,
    norm_attn,
    w_qkv,
    w_attn_out,
    norm_conv,
    w_point_in,
    w_depth,
    w_point_out,
    w_adapter,
    llm_gain,
    w_query,
    w_key,
    w_value,
):
    mp_count = lax.axis_size("mp")
    frame_rows, width = frames.shape
    heads = CH
    head_size = width // heads
    shard_frames = frame_rows * mp_count
    time_place = lax.axis_index("tm")
    model_place = lax.axis_index("mp")
    first = (time_place * mp_count + model_place) * frame_rows
    inputs = frames.astype(jnp.float32)
    own_index = first + jnp.arange(frame_rows, dtype=jnp.int32)
    own_place, own_count = shard_count(own_index, valid_counts, shard_frames)
    frame_real = own_place < own_count
    normed = layer_norm(inputs, norm_attn).astype(jnp.bfloat16)
    projected = jnp.dot(normed, w_qkv, preferred_element_type=jnp.float32).astype(jnp.bfloat16)
    queries = projected[:, :width]
    own_keys = projected[:, width : 2 * width]
    own_values = projected[:, 2 * width :]
    prior_keys, prior_values = passed_along((own_keys, own_values), ("tm", "mp"), 1)
    keys = jnp.concatenate([prior_keys, own_keys], axis=0).reshape(2 * frame_rows, heads, head_size)
    values = jnp.concatenate([prior_values, own_values], axis=0).reshape(
        2 * frame_rows, heads, head_size
    )
    key_index = first - frame_rows + jnp.arange(2 * frame_rows, dtype=jnp.int32)
    key_place, key_count = shard_count(key_index, valid_counts, shard_frames)
    key_real = key_place < key_count
    prior_ids = lax.dynamic_slice_in_dim(
        block_ids, jnp.maximum(first - frame_rows, 0), frame_rows, 0
    )
    query_ids = lax.dynamic_slice_in_dim(block_ids, first, frame_rows, 0)
    key_ids = jnp.concatenate([prior_ids, query_ids], axis=0)
    same = key_index[None, :] == own_index[:, None]
    visible = (
        (key_index[None, :] <= own_index[:, None])
        & (key_ids[None, :] >= query_ids[:, None] - 2)
        & (key_real[None, :] | same)
    )
    query_heads = queries.reshape(frame_rows, heads, head_size)
    scores = jnp.einsum(
        "qhd,khd->hqk", query_heads, keys, preferred_element_type=jnp.float32
    ) / jnp.sqrt(jnp.float32(head_size))
    scores = jnp.where(visible[None], scores, masked_score)
    top = jnp.max(scores, axis=-1, keepdims=True)
    weights = jnp.where(visible[None], jnp.exp(scores - top), 0.0)
    total = jnp.sum(weights, axis=-1)
    summed = jnp.einsum(
        "hqk,khd->qhd", weights.astype(jnp.bfloat16), values, preferred_element_type=jnp.float32
    )
    conf_context = (
        (summed / jnp.transpose(total)[:, :, None]).reshape(frame_rows, width).astype(jnp.bfloat16)
    )
    mid = inputs + jnp.dot(conf_context, w_attn_out, preferred_element_type=jnp.float32)
    conv_in = layer_norm(mid, norm_conv).astype(jnp.bfloat16)
    both = jnp.dot(conv_in, w_point_in, preferred_element_type=jnp.float32)
    glu = both[:, :width] * jax.nn.sigmoid(both[:, width:])
    glu = jnp.where(frame_real[:, None], glu, 0.0).astype(jnp.bfloat16)
    taps = w_depth.shape[0]
    rim = passed_along(glu[frame_rows - (taps - 1) :], ("tm", "mp"), 1)
    padded = jnp.concatenate([rim, glu], axis=0).astype(jnp.float32)
    kernel = w_depth.astype(jnp.float32)
    depth = jnp.zeros((frame_rows, width), jnp.float32)
    for tap in range(taps):
        depth = depth + kernel[tap][None, :] * padded[taps - 1 - tap : taps - 1 - tap + frame_rows]
    activated = jax.nn.silu(depth).astype(jnp.bfloat16)
    final = mid + jnp.dot(activated, w_point_out, preferred_element_type=jnp.float32)
    conf_out = jnp.where(frame_real[:, None], final, 0.0).astype(jnp.bfloat16)
    pooled = (
        jnp.sum(conf_out.astype(jnp.float32).reshape(frame_rows // 4, 4, width), axis=1) * 0.25
    ).astype(jnp.bfloat16)
    shard_pooled = lax.all_gather(pooled, "mp", axis=0, tiled=True)
    shard_tokens = shard_pooled.shape[0]
    adapter_part = lax.all_gather(w_adapter, "tm", axis=0, tiled=True)
    adapter_full = lax.all_gather(adapter_part, "mp", axis=1, tiled=True)
    adapted = jnp.dot(shard_pooled, adapter_full, preferred_element_type=jnp.float32)
    llm_in = (
        adapted
        * lax.rsqrt(jnp.mean(adapted * adapted, axis=-1, keepdims=True) + eps_llm)
        * llm_gain
    ).astype(jnp.bfloat16)
    query_cols = w_query.shape[1]
    key_cols = w_key.shape[1]
    raw_query = jnp.dot(
        llm_in,
        lax.all_gather(w_query, "tm", axis=0, tiled=True),
        preferred_element_type=jnp.float32,
    )
    raw_keys = jnp.dot(
        llm_in, lax.all_gather(w_key, "tm", axis=0, tiled=True), preferred_element_type=jnp.float32
    )
    raw_values = jnp.dot(
        llm_in,
        lax.all_gather(w_value, "tm", axis=0, tiled=True),
        preferred_element_type=jnp.float32,
    )
    llm_size = HDIM
    query_heads_dev = query_cols // llm_size
    kv_heads = key_cols // llm_size
    group = query_heads_dev // kv_heads
    token_index = time_place * shard_tokens + jnp.arange(shard_tokens, dtype=jnp.int32)
    llm_query = rotary(
        raw_query.reshape(shard_tokens, query_heads_dev, llm_size), token_index
    ).astype(jnp.bfloat16)
    llm_query = llm_query.reshape(shard_tokens, kv_heads, group, llm_size)
    llm_keys = (
        rotary(raw_keys.reshape(shard_tokens, kv_heads, llm_size), token_index)
        .astype(jnp.bfloat16)
        .reshape(shard_tokens, key_cols)
    )
    llm_values = raw_values.astype(jnp.bfloat16)
    score_scale = 1.0 / jnp.sqrt(jnp.float32(llm_size))
    start_state = (
        jnp.full((kv_heads, group, shard_tokens), masked_score, jnp.float32),
        jnp.zeros((kv_heads, group, shard_tokens), jnp.float32),
        jnp.zeros((kv_heads, group, shard_tokens, llm_size), jnp.float32),
    )
    key_piece = lax.all_gather(llm_keys, "tm", axis=0, tiled=True)
    value_piece = lax.all_gather(llm_values, "tm", axis=0, tiled=True)
    piece_rows = key_piece.shape[0]
    step_rows = math.gcd(piece_rows, 512)

    def one_step(block, state):
        best, total_weight, accum = state
        key_block = lax.dynamic_slice_in_dim(key_piece, block * step_rows, step_rows, 0).reshape(
            step_rows, kv_heads, llm_size
        )
        value_block = lax.dynamic_slice_in_dim(
            value_piece, block * step_rows, step_rows, 0
        ).reshape(step_rows, kv_heads, llm_size)
        block_index = block * step_rows + jnp.arange(step_rows, dtype=jnp.int32)
        block_place, block_count = shard_count(block_index, valid_counts, shard_tokens)
        block_real = block_place * 4 < block_count
        matches = block_index[None, :] == token_index[:, None]
        seen = (block_index[None, :] <= token_index[:, None]) & (block_real[None, :] | matches)
        block_scores = (
            jnp.einsum("qhgd,khd->hgqk", llm_query, key_block, preferred_element_type=jnp.float32)
            * score_scale
        )
        block_scores = jnp.where(seen[None, None], block_scores, masked_score)
        new_best = jnp.maximum(best, jnp.max(block_scores, axis=-1))
        block_weights = jnp.where(
            seen[None, None], jnp.exp(block_scores - new_best[..., None]), 0.0
        )
        fade = jnp.exp(best - new_best)
        total_weight = total_weight * fade + jnp.sum(block_weights, axis=-1)
        accum = accum * fade[..., None] + jnp.einsum(
            "hgqk,khd->hgqd",
            block_weights.astype(jnp.bfloat16),
            value_block,
            preferred_element_type=jnp.float32,
        )
        return (new_best, total_weight, accum)

    best, total_weight, accum = lax.fori_loop(0, piece_rows // step_rows, one_step, start_state)
    result = accum / total_weight[..., None]
    attended = (
        jnp.transpose(result, (2, 0, 1, 3)).reshape(shard_tokens, query_cols).astype(jnp.bfloat16)
    )
    return (conf_out, attended)


def solution(mesh):
    placed = (
        P(("tm", "mp"), None),
        P(),
        P(),
        P(),
        P(),
        P(),
        P(),
        P(),
        P(),
        P(),
        P("tm", "mp"),
        P(),
        P("tm", "mp"),
        P("tm", "mp"),
        P("tm", "mp"),
    )
    return jax.shard_map(
        on_device,
        mesh=mesh,
        in_specs=placed,
        out_specs=(P(("tm", "mp"), None), P("tm", "mp")),
        check_vma=False,
    )
```

profile of v0, /device:TPU:0, one launch (start us, length us, event | category | flops | bytes accessed | tf_op | source)
XLA Modules:
  0.0 644.8 jit_solution(2328061743884182033)
XLA Ops:
  8.0 41.4 %all-gather.6.cloned.1.call-done = bf16[1024,2048]{1,0:T(8,128)(2,1)} async-done(((bf16[128,2048]{1,0:T(8,128)(2,1)}), bf16[1024,2048]{1,0:T(8,128)(2,1)}) %all-gather.6.cloned.1.call-update) | async-done | bytes 4194320 | tf_op jit(solution)/shard_map/all_gather | solution.py:132
  51.7 3.9 convolution_convert_fusion
  56.3 3.4 collective-permute-start.1
  59.7 4.1 collective-permute-start
  69.6 10.4 %collective-permute-done = bf16[128,1024]{1,0:T(8,128)(2,1)} collective-permute-done((bf16[128,1024]{1,0:T(8,128)(2,1)}, bf16[128,1024]{1,0:T(8,128)(2,1)}, u32[]{:S(2)}, u32[]{:S(2)}) %collective-permute-start) | collective-permute-done | bytes 262176 | tf_op jit(solution)/shard_map/ppermute | solution.py:18
  82.1 2.0 fusion.95
  86.0 3.9 fusion.22
  91.0 3.1 fusion.72
  94.3 13.2 %collective-permute-start.2 = (bf16[30,1024]{1,0:T(8,128)(2,1)S(1)}, bf16[30,1024]{1,0:T(8,128)(2,1)S(1)}, u32[]{:S(2)}, u32[]{:S(2)}) collective-permute-start(bf16[30,1024]{1,0:T(8,128)(2,1)S(1)} %slice.294), channel_id=1, source_target_pairs={{0,1},{1,2},{2,3},{3,4},{4,5},{5,6},{6,7},{7,8},{8,9},{9,10},{10,1... | collective-permute-start | bytes 184328 | tf_op jit(solution)/shard_map/ppermute | solution.py:18
  107.6 3.0 collective-permute-done.2
  111.1 2.5 fusion.23
  114.1 36.5 %all_gather.24 = bf16[128,1024]{1,0:T(8,128)(2,1)S(1)} all-gather(bf16[32,1024]{1,0:T(8,128)(2,1)S(1)} %multiply_convert_fusion.5), channel_id=1, replica_groups=mesh['tm'=8,'mp'=4] {'mp'}, dimensions={0}, use_global_device_ids=true | all-gather | bytes 327680 | tf_op jit(solution)/shard_map/all_gather | solution.py:130
  150.6 200.2 %all-gather.8.cloned.1.call-done = bf16[1024,8192]{1,0:T(8,128)(2,1)} async-done(((bf16[1024,2048]{1,0:T(8,128)(2,1)}), bf16[1024,8192]{1,0:T(8,128)(2,1)}) %all-gather.8.cloned.1.call-update) | async-done | bytes 16777232 | tf_op jit(solution)/shard_map/all_gather | solution.py:133
  350.8 8.2 %multiply_reduce_fusion = (f32[128]{0:T(128)S(1)}, f32[128,8192]{1,0:T(8,128)S(1)}) fusion(bf16[128,1024]{1,0:T(8,128)(2,1)S(1)} %all_gather.24, bf16[1024,8192]{1,0:T(8,128)(2,1)} %all-gather.8.cloned.1.call-done), kind=kOutput, calls=%fused_computation.35 | convolution fusion | flops 2149580800 | bytes 21234176 | tf_op jit(solution)/shard_map/dot_general | solution.py:134
  359.5 27.4 %all-gather.10.cloned.1.call-done = bf16[8192,256]{1,0:T(8,128)(2,1)} async-done(((bf16[1024,256]{1,0:T(8,128)(2,1)}), bf16[8192,256]{1,0:T(8,128)(2,1)}) %all-gather.10.cloned.1.call-update) | async-done | bytes 4194320 | tf_op jit(solution)/shard_map/all_gather | solution.py:148
  386.9 2.9 fusion.98
  390.4 12.2 %all_gather.28 = bf16[1024,256]{1,0:T(8,128)(2,1)} all-gather(bf16[128,256]{1,0:T(8,128)(2,1)S(1)} %fusion.82), channel_id=1, replica_groups=mesh['tm'=8,'mp'=4] {'tm'}, dimensions={0}, use_global_device_ids=true | all-gather | bytes 589824 | tf_op jit(solution)/shard_map/all_gather | solution.py:176
  402.6 23.5 %all-gather.14.cloned.1.call-done = bf16[8192,256]{1,0:T(8,128)(2,1)} async-done(((bf16[1024,256]{1,0:T(8,128)(2,1)}), bf16[8192,256]{1,0:T(8,128)(2,1)}) %all-gather.14.cloned.1.call-update) | async-done | bytes 4194320 | tf_op jit(solution)/shard_map/all_gather | solution.py:152
  426.1 2.9 convolution_convert_fusion.1
  429.0 10.8 %all_gather.31 = bf16[1024,256]{1,0:T(8,128)(2,1)} all-gather(bf16[128,256]{1,0:T(8,128)(2,1)S(1)} %convolution_convert_fusion.1), channel_id=1, replica_groups=mesh['tm'=8,'mp'=4] {'tm'}, dimensions={0}, use_global_device_ids=true | all-gather | bytes 589824 | tf_op jit(solution)/shard_map/all_gather | solution.py:177
  439.8 148.9 %all-gather.12.cloned.1.call-done = bf16[8192,2048]{1,0:T(8,128)(2,1)} async-done(((bf16[1024,2048]{1,0:T(8,128)(2,1)}), bf16[8192,2048]{1,0:T(8,128)(2,1)}) %all-gather.12.cloned.1.call-update) | async-done | bytes 33554448 | tf_op jit(solution)/shard_map/all_gather | solution.py:144
  588.7 12.9 %fusion.99 = f32[128,2048]{1,0:T(8,128)S(1)} fusion(bf16[128,8192]{1,0:T(8,128)(2,1)S(1)} %multiply_convert_fusion, bf16[8192,2048]{1,0:T(8,128)(2,1)} %all-gather.12.cloned.1.call-done), kind=kOutput, calls=%fused_computation.199 | convolution fusion | flops 4294967296 | bytes 36700160 | tf_op jit(solution)/shard_map/dot_general | solution.py:142
  603.0 2.4 copy.57
  605.4 2.4 copy.58
  608.0 2.2 fusion.25
  610.2 25.0 %while.20 = (s32[]{:T(128)}, f32[2,8,128]{2,1,0:T(8,128)S(1)}, f32[2,8,128]{2,1,0:T(8,128)S(1)}, f32[2,8,128,128]{3,2,1,0:T(8,128)}, s32[8]{0:T(128)S(1)}, /*ind...) while((s32[]{:T(128)}, f32[2,8,128]{2,1,0:T(8,128)S(1)}, ...), condition=%wide.region_14.15_spmd.clone, body=%wide.region_10.14_spmd.clone.sunk | while | flops 551591552 | bytes 26622240 | solution.py:213
  611.7 2.8 fusion.133
  614.6 3.2 fusion.134
  617.9 3.9 fusion.136
  624.3 2.8 fusion.133
  627.1 3.2 fusion.134
  630.4 3.9 fusion.136
  (184 shorter events, 26.0 us)
Async XLA Ops:
  7.2 82.7 %copy-start = (bf16[1024,1024]{1,0:T(8,128)(2,1)S(1)}, bf16[1024,1024]{1,0:T(8,128)(2,1)}, u32[]{:S(2)}) copy-start(bf16[1024,1024]{1,0:T(8,128)(2,1)} %param.22) | copy-start | bytes 6291460
  7.2 42.2 %all-gather.6.cloned.1.call-start = ((), (), s32[]{:S(2)}) async-start(), calls=%async_computation | async-start | bytes 4718592 | tf_op jit(solution)/shard_map/all_gather | solution.py:132
  7.9 342.8 %all-gather.8.cloned.1.call-start = ((), (), s32[]{:S(2)}) async-start(), calls=%async_computation.1 | async-start | bytes 20971520 | tf_op jit(solution)/shard_map/all_gather | solution.py:133
  49.4 337.5 %all-gather.10.cloned.1.call-start = ((), (), s32[]{:S(2)}) async-start(), calls=%async_computation.2 | async-start | bytes 4718592 | tf_op jit(solution)/shard_map/all_gather | solution.py:148
  50.1 376.0 %all-gather.14.cloned.1.call-start = ((), (), s32[]{:S(2)}) async-start(), calls=%async_computation.4 | async-start | bytes 4718592 | tf_op jit(solution)/shard_map/all_gather | solution.py:152
  50.7 538.0 %all-gather.12.cloned.1.call-start = ((), (), s32[]{:S(2)}) async-start(), calls=%async_computation.3 | async-start | bytes 37748736 | tf_op jit(solution)/shard_map/all_gather | solution.py:144
  56.3 13.0 %collective-permute-start.1 = (bf16[128,1024]{1,0:T(8,128)(2,1)S(1)}, bf16[128,1024]{1,0:T(8,128)(2,1)S(1)}, u32[]{:S(2)}, u32[]{:S(2)}) collective-permute-start(bf16[128,1024]{1,0:T(8,128)(2,1)S(1)} %get-tuple-element.316), channel_id=1, source_target_pairs={{0,1},{1,2},{2,3},{3,4},{4,5},{5,6},{6,7},{7,8},{8,9},{9,10},{10,1... | collective-permute-start | bytes 786440 | tf_op jit(solution)/shard_map/ppermute | solution.py:18
  59.7 20.3 %collective-permute-start = (bf16[128,1024]{1,0:T(8,128)(2,1)}, bf16[128,1024]{1,0:T(8,128)(2,1)}, u32[]{:S(2)}, u32[]{:S(2)}) collective-permute-start(bf16[128,1024]{1,0:T(8,128)(2,1)} %get-tuple-element.318), channel_id=1, source_target_pairs={{0,1},{1,2},{2,3},{3,4},{4,5},{5,6},{6,7},{7,8},{8,9},{9,10},{10,1... | collective-permute-start | bytes 786440 | tf_op jit(solution)/shard_map/ppermute | solution.py:18
  90.6 20.1 %copy-start.13 = (f32[1,1024]{1,0:T(1,128)S(1)}, f32[1,1024]{1,0:T(1,128)}, u32[]{:S(2)}) copy-start(f32[1,1024]{1,0:T(1,128)} %get-tuple-element.340) | copy-start | bytes 12292
  90.7 20.1 %copy-start.14 = (f32[1,1024]{1,0:T(1,128)S(1)}, f32[1,1024]{1,0:T(1,128)}, u32[]{:S(2)}) copy-start(f32[1,1024]{1,0:T(1,128)} %get-tuple-element.341) | copy-start | bytes 12292
  90.7 20.1 %copy-start.15 = (f32[1,1024]{1,0:T(1,128)S(1)}, f32[1,1024]{1,0:T(1,128)}, u32[]{:S(2)}) copy-start(f32[1,1024]{1,0:T(1,128)} %get-tuple-element.342) | copy-start | bytes 12292
  90.7 20.1 %copy-start.16 = (f32[1,1024]{1,0:T(1,128)S(1)}, f32[1,1024]{1,0:T(1,128)}, u32[]{:S(2)}) copy-start(f32[1,1024]{1,0:T(1,128)} %get-tuple-element.343) | copy-start | bytes 12292
  90.7 20.1 %copy-start.17 = (f32[1,1024]{1,0:T(1,128)S(1)}, f32[1,1024]{1,0:T(1,128)}, u32[]{:S(2)}) copy-start(f32[1,1024]{1,0:T(1,128)} %get-tuple-element.344) | copy-start | bytes 12292
  90.7 20.1 %copy-start.18 = (f32[1,1024]{1,0:T(1,128)S(1)}, f32[1,1024]{1,0:T(1,128)}, u32[]{:S(2)}) copy-start(f32[1,1024]{1,0:T(1,128)} %get-tuple-element.345) | copy-start | bytes 12292
  90.7 20.1 %copy-start.19 = (f32[1,1024]{1,0:T(1,128)S(1)}, f32[1,1024]{1,0:T(1,128)}, u32[]{:S(2)}) copy-start(f32[1,1024]{1,0:T(1,128)} %get-tuple-element.346) | copy-start | bytes 12292
  90.7 20.1 %copy-start.20 = (f32[1,1024]{1,0:T(1,128)S(1)}, f32[1,1024]{1,0:T(1,128)}, u32[]{:S(2)}) copy-start(f32[1,1024]{1,0:T(1,128)} %get-tuple-element.347) | copy-start | bytes 12292
  90.7 20.1 %copy-start.21 = (f32[1,1024]{1,0:T(1,128)S(1)}, f32[1,1024]{1,0:T(1,128)}, u32[]{:S(2)}) copy-start(f32[1,1024]{1,0:T(1,128)} %get-tuple-element.348) | copy-start | bytes 12292
  90.7 20.1 %copy-start.22 = (f32[1,1024]{1,0:T(1,128)S(1)}, f32[1,1024]{1,0:T(1,128)}, u32[]{:S(2)}) copy-start(f32[1,1024]{1,0:T(1,128)} %get-tuple-element.349) | copy-start | bytes 12292
  90.7 20.1 %copy-start.23 = (f32[1,1024]{1,0:T(1,128)S(1)}, f32[1,1024]{1,0:T(1,128)}, u32[]{:S(2)}) copy-start(f32[1,1024]{1,0:T(1,128)} %get-tuple-element.350) | copy-start | bytes 12292
  90.8 20.1 %copy-start.24 = (f32[1,1024]{1,0:T(1,128)S(1)}, f32[1,1024]{1,0:T(1,128)}, u32[]{:S(2)}) copy-start(f32[1,1024]{1,0:T(1,128)} %get-tuple-element.351) | copy-start | bytes 12292
  90.8 20.1 %copy-start.25 = (f32[1,1024]{1,0:T(1,128)S(1)}, f32[1,1024]{1,0:T(1,128)}, u32[]{:S(2)}) copy-start(f32[1,1024]{1,0:T(1,128)} %get-tuple-element.321) | copy-start | bytes 12292
  90.8 20.1 %copy-start.26 = (f32[1,1024]{1,0:T(1,128)S(1)}, f32[1,1024]{1,0:T(1,128)}, u32[]{:S(2)}) copy-start(f32[1,1024]{1,0:T(1,128)} %get-tuple-element.322) | copy-start | bytes 12292
  90.8 20.1 %copy-start.27 = (f32[1,1024]{1,0:T(1,128)S(1)}, f32[1,1024]{1,0:T(1,128)}, u32[]{:S(2)}) copy-start(f32[1,1024]{1,0:T(1,128)} %get-tuple-element.323) | copy-start | bytes 12292
  90.8 20.1 %copy-start.28 = (f32[1,1024]{1,0:T(1,128)S(1)}, f32[1,1024]{1,0:T(1,128)}, u32[]{:S(2)}) copy-start(f32[1,1024]{1,0:T(1,128)} %get-tuple-element.324) | copy-start | bytes 12292
  90.8 20.1 %copy-start.29 = (f32[1,1024]{1,0:T(1,128)S(1)}, f32[1,1024]{1,0:T(1,128)}, u32[]{:S(2)}) copy-start(f32[1,1024]{1,0:T(1,128)} %get-tuple-element.325) | copy-start | bytes 12292
  90.8 20.1 %copy-start.30 = (f32[1,1024]{1,0:T(1,128)S(1)}, f32[1,1024]{1,0:T(1,128)}, u32[]{:S(2)}) copy-start(f32[1,1024]{1,0:T(1,128)} %get-tuple-element.326) | copy-start | bytes 12292
  90.8 20.1 %copy-start.31 = (f32[1,1024]{1,0:T(1,128)S(1)}, f32[1,1024]{1,0:T(1,128)}, u32[]{:S(2)}) copy-start(f32[1,1024]{1,0:T(1,128)} %get-tuple-element.327) | copy-start | bytes 12292
  90.8 20.1 %copy-start.32 = (f32[1,1024]{1,0:T(1,128)S(1)}, f32[1,1024]{1,0:T(1,128)}, u32[]{:S(2)}) copy-start(f32[1,1024]{1,0:T(1,128)} %get-tuple-element.328) | copy-start | bytes 12292
  90.8 20.1 %copy-start.33 = (f32[1,1024]{1,0:T(1,128)S(1)}, f32[1,1024]{1,0:T(1,128)}, u32[]{:S(2)}) copy-start(f32[1,1024]{1,0:T(1,128)} %get-tuple-element.329) | copy-start | bytes 12292
  94.3 16.3 %collective-permute-start.2 = (bf16[30,1024]{1,0:T(8,128)(2,1)S(1)}, bf16[30,1024]{1,0:T(8,128)(2,1)S(1)}, u32[]{:S(2)}, u32[]{:S(2)}) collective-permute-start(bf16[30,1024]{1,0:T(8,128)(2,1)S(1)} %slice.294), channel_id=1, source_target_pairs={{0,1},{1,2},{2,3},{3,4},{4,5},{5,6},{6,7},{7,8},{8,9},{9,10},{10,1... | collective-permute-start | bytes 184328 | tf_op jit(solution)/shard_map/ppermute | solution.py:18
  113.6 245.4 %copy-start.7 = (bf16[128,1024]{1,0:T(8,128)(2,1)}, bf16[128,1024]{1,0:T(8,128)(2,1)S(1)}, u32[]{:S(2)}) copy-start(bf16[128,1024]{1,0:T(8,128)(2,1)S(1)} %fusion.23) | copy-start | bytes 786436
  150.6 208.4 %copy-start.10 = (f32[8192]{0:T(1024)S(1)}, f32[8192]{0:T(1024)}, u32[]{:S(2)}) copy-start(f32[8192]{0:T(1024)} %param.28) | copy-start | bytes 98308
  (25 other events, 295.1 us)
Sparse Core Ops, SparseCore 0:
  9.9 39.4 all-gather.5
  50.9 299.7 all-gather.7
  352.7 34.2 all-gather.9
  388.7 37.3 all-gather.13
  427.8 160.7 all-gather.11
where the time goes:
time: 646 us; the launch traced here: 645 us
  waiting for transfers between devices  458 us (71%)
  blocking collectives  59.4 us (9%)
  matrix products  58.1 us (9%)
  starting transfers between devices  20.9 us (3%)
  other arithmetic  18.1 us (3%)
  local copies, waits for them, and re-layouts  15.7 us (2%)
  between operations  14.7 us (2%)
    all_gather x1, waiting for transfers between devices, on_device(): adapter_full = lax.all_gather(adapter_part, 'mp', axis=1, tiled=True)  200 us
    all_gather x1, waiting for transfers between devices, on_device(): lax.all_gather(w_query, 'tm', axis=0, tiled=True)  149 us
    all_gather x1, waiting for transfers between devices, on_device(): adapter_part = lax.all_gather(w_adapter, 'tm', axis=0, tiled=True)  41.4 us
    all_gather x1, blocking collectives, on_device(): shard_pooled = lax.all_gather(pooled, 'mp', axis=0, tiled=True)  36.5 us
    all_gather x1, waiting for transfers between devices, on_device(): lax.all_gather(w_key, 'tm', axis=0, tiled=True)  27.4 us
    all_gather x1, waiting for transfers between devices, on_device(): lax.all_gather(w_value, 'tm', axis=0, tiled=True)  23.5 us
    ppermute x3, starting transfers between devices, passed_along(): return lax.ppermute(value, axis, pairs)  20.7 us
    ppermute x3, waiting for transfers between devices, passed_along(): return lax.ppermute(value, axis, pairs)  14.1 us
  transfers between devices with their start and end apart: 8, of which 8 were waited for; matrix products, arithmetic and copies ran while one was open for 7% of the time, Pallas kernels for 0%

commit v1 on v0

--- a/solution.py
+++ b/solution.py
@@ -10,6 +10,16 @@
 eps_llm = 1e-06
 rope_base = 1000000.0
 masked_score = -1e30
+
+
+def draw_the_series_all(original, matrix, mesh_ax):
+    return jnp.split(
+        jax.lax.all_gather(
+            jnp.concatenate([original, matrix], axis=1), axis_name=mesh_ax, axis=0, tiled=True
+        ),
+        [original.shape[1]],
+        axis=1,
+    )
 
 
 def passed_along(value, axis, by):
@@ -173,8 +183,7 @@
         jnp.zeros((kv_heads, group, shard_tokens), jnp.float32),
         jnp.zeros((kv_heads, group, shard_tokens, llm_size), jnp.float32),
     )
-    key_piece = lax.all_gather(llm_keys, "tm", axis=0, tiled=True)
-    value_piece = lax.all_gather(llm_values, "tm", axis=0, tiled=True)
+    key_piece, value_piece = draw_the_series_all(llm_keys, llm_values, "tm")
     piece_rows = key_piece.shape[0]
     step_rows = math.gcd(piece_rows, 512)
 

time: 646 us -> 671 us (1.039)
  waiting for transfers between devices: 458 us -> 514 us
  blocking collectives: 59.4 us -> 25.4 us
    all_gather x0 -> x1, waiting for transfers between devices: none -> 23 us  [draw_the_series_all(): jax.lax.all_gather(jnp.concatenate([original, matrix], axis=1), axis_name...]
    all_gather x2 -> x0, blocking collectives: 23 us -> none  [the longest x1 12.2 us: on_device(): key_piece = lax.all_gather(llm_keys, 'tm', axis=0, tiled=True)]
    all_gather x1, waiting for transfers between devices: 200 us -> 216 us  [on_device(): adapter_full = lax.all_gather(adapter_part, 'mp', axis=1, tiled=True)]
    all_gather x1, waiting for transfers between devices: 149 us -> 160 us  [on_device(): lax.all_gather(w_query, 'tm', axis=0, tiled=True)]
    all_gather x1, waiting for transfers between devices: 23.5 us -> 35 us  [on_device(): lax.all_gather(w_value, 'tm', axis=0, tiled=True)]
    all_gather x1, blocking collectives: 36.5 us -> 25.4 us  [on_device(): shard_pooled = lax.all_gather(pooled, 'mp', axis=0, tiled=True)]
  transfers between devices with their start and end apart: 8 -> 9, of which waited for: 8 -> 8; matrix products, arithmetic and copies ran while one was open for 7% -> 6% of each run, Pallas kernels for 0% -> 0%
where the time goes in v1:
time: 671 us
  waiting for transfers between devices  514 us (77%)
  matrix products  59.6 us (9%)
  blocking collectives  25.4 us (4%)
  starting transfers between devices  21 us (3%)
  other arithmetic  18.2 us (3%)
  local copies, waits for them, and re-layouts  17.2 us (3%)
  between operations  15.1 us (2%)
    all_gather x1, waiting for transfers between devices, on_device(): adapter_full = lax.all_gather(adapter_part, 'mp', axis=1, tiled=True)  216 us
    all_gather x1, waiting for transfers between devices, on_device(): lax.all_gather(w_query, 'tm', axis=0, tiled=True)  160 us
    all_gather x1, waiting for transfers between devices, on_device(): adapter_part = lax.all_gather(w_adapter, 'tm', axis=0, tiled=True)  41.4 us
    all_gather x1, waiting for transfers between devices, on_device(): lax.all_gather(w_value, 'tm', axis=0, tiled=True)  35 us
    all_gather x1, waiting for transfers between devices, on_device(): lax.all_gather(w_key, 'tm', axis=0, tiled=True)  27.3 us
    all_gather x1, blocking collectives, on_device(): shard_pooled = lax.all_gather(pooled, 'mp', axis=0, tiled=True)  25.4 us
    all_gather x1, waiting for transfers between devices, draw_the_series_all(): jax.lax.all_gather(jnp.concatenate([original, matrix], axis=1), axis_name...  23 us
    ppermute x3, starting transfers between devices, passed_along(): return lax.ppermute(value, axis, pairs)  20.8 us
  transfers between devices with their start and end apart: 9, of which 8 were waited for; matrix products, arithmetic and copies ran while one was open for 6% of the time, Pallas kernels for 0%

profile of v1, /device:TPU:0, one launch (start us, length us, event | category | flops | bytes accessed | tf_op | source)
XLA Modules:
  0.0 670.6 jit_solution(2148825326402051639)
XLA Ops:
  8.0 41.4 %all-gather.7.cloned.1.call-done = bf16[1024,2048]{1,0:T(8,128)(2,1)} async-done(((bf16[128,2048]{1,0:T(8,128)(2,1)}), bf16[1024,2048]{1,0:T(8,128)(2,1)}) %all-gather.7.cloned.1.call-update) | async-done | bytes 4194320 | tf_op jit(solution)/shard_map/all_gather | solution.py:142
  50.6 3.9 convolution_convert_fusion
  55.2 3.4 collective-permute-start.1
  58.6 4.1 collective-permute-start
  67.5 2.8 fusion.98
  72.2 5.5 collective-permute-done
  79.1 3.8 fusion.22
  84.0 3.1 fusion.72
  87.3 13.3 %collective-permute-start.2 = (bf16[30,1024]{1,0:T(8,128)(2,1)S(1)}, bf16[30,1024]{1,0:T(8,128)(2,1)S(1)}, u32[]{:S(2)}, u32[]{:S(2)}) collective-permute-start(bf16[30,1024]{1,0:T(8,128)(2,1)S(1)} %slice.294), channel_id=1, source_target_pairs={{0,1},{1,2},{2,3},{3,4},{4,5},{5,6},{6,7},{7,8},{8,9},{9,10},{10,1... | collective-permute-start | bytes 184328 | tf_op jit(solution)/shard_map/ppermute | solution.py:28
  100.7 3.0 collective-permute-done.2
  104.1 3.2 fusion.23
  107.9 25.4 %all_gather.21 = bf16[128,1024]{1,0:T(8,128)(2,1)S(1)} all-gather(bf16[32,1024]{1,0:T(8,128)(2,1)S(1)} %multiply_convert_fusion.5), channel_id=1, replica_groups=mesh['tm'=8,'mp'=4] {'mp'}, dimensions={0}, use_global_device_ids=true | all-gather | bytes 327680 | tf_op jit(solution)/shard_map/all_gather | solution.py:140
  133.3 216.4 %all-gather.9.cloned.1.call-done = bf16[1024,8192]{1,0:T(8,128)(2,1)} async-done(((bf16[1024,2048]{1,0:T(8,128)(2,1)}), bf16[1024,8192]{1,0:T(8,128)(2,1)}) %all-gather.9.cloned.1.call-update) | async-done | bytes 16777232 | tf_op jit(solution)/shard_map/all_gather | solution.py:143
  349.7 8.2 %multiply_reduce_fusion = (f32[128]{0:T(128)S(1)}, f32[128,8192]{1,0:T(8,128)S(1)}) fusion(bf16[128,1024]{1,0:T(8,128)(2,1)S(1)} %all_gather.21, bf16[1024,8192]{1,0:T(8,128)(2,1)} %all-gather.9.cloned.1.call-done), kind=kOutput, calls=%fused_computation.35 | convolution fusion | flops 2149580800 | bytes 21234176 | tf_op jit(solution)/shard_map/dot_general | solution.py:144
  358.4 27.3 %all-gather.11.cloned.1.call-done = bf16[8192,256]{1,0:T(8,128)(2,1)} async-done(((bf16[1024,256]{1,0:T(8,128)(2,1)}), bf16[8192,256]{1,0:T(8,128)(2,1)}) %all-gather.11.cloned.1.call-update) | async-done | bytes 4194320 | tf_op jit(solution)/shard_map/all_gather | solution.py:158
  385.8 2.9 fusion.99
  389.3 35.0 %all-gather.13.cloned.1.call-done = bf16[8192,256]{1,0:T(8,128)(2,1)} async-done(((bf16[1024,256]{1,0:T(8,128)(2,1)}), bf16[8192,256]{1,0:T(8,128)(2,1)}) %all-gather.13.cloned.1.call-update) | async-done | bytes 4194320 | tf_op jit(solution)/shard_map/all_gather | solution.py:162
  424.3 2.9 convolution_convert_fusion.1
  428.5 23.0 %all-gather.15.cloned.1.call-done = bf16[1024,512]{1,0:T(8,128)(2,1)} async-done(((bf16[128,512]{1,0:T(8,128)(2,1)}), bf16[1024,512]{1,0:T(8,128)(2,1)}) %all-gather.15.cloned.1.call-update) | async-done | bytes 1048592 | tf_op jit(solution)/shard_map/all_gather | solution.py:17
  451.5 2.2 fusion.92
  453.7 160.3 %all-gather.17.cloned.1.call-done = bf16[8192,2048]{1,0:T(8,128)(2,1)} async-done(((bf16[1024,2048]{1,0:T(8,128)(2,1)}), bf16[8192,2048]{1,0:T(8,128)(2,1)}) %all-gather.17.cloned.1.call-update) | async-done | bytes 33554448 | tf_op jit(solution)/shard_map/all_gather | solution.py:154
  614.1 12.9 %fusion.100 = f32[128,2048]{1,0:T(8,128)S(1)} fusion(bf16[128,8192]{1,0:T(8,128)(2,1)S(1)} %multiply_convert_fusion, bf16[8192,2048]{1,0:T(8,128)(2,1)} %all-gather.17.cloned.1.call-done), kind=kOutput, calls=%fused_computation.201 | convolution fusion | flops 4294967296 | bytes 36700160 | tf_op jit(solution)/shard_map/dot_general | solution.py:152
  628.4 2.4 copy.57
  630.8 2.4 copy.58
  633.4 2.2 fusion.25
  635.7 25.1 %while.20 = (s32[]{:T(128)}, f32[2,8,128]{2,1,0:T(8,128)S(1)}, f32[2,8,128]{2,1,0:T(8,128)S(1)}, f32[2,8,128,128]{3,2,1,0:T(8,128)}, s32[8]{0:T(128)S(1)}, /*ind...) while((s32[]{:T(128)}, f32[2,8,128]{2,1,0:T(8,128)S(1)}, ...), condition=%wide.region_14.15_spmd.clone, body=%wide.region_10.14_spmd.clone.sunk | while | flops 551591552 | bytes 26622240 | solution.py:222
  637.2 2.8 fusion.134
  640.0 3.2 fusion.135
  643.4 3.9 fusion.137
  649.7 2.8 fusion.134
  652.5 3.2 fusion.135
  655.9 3.9 fusion.137
  (185 shorter events, 24.4 us)
Async XLA Ops:
  7.2 75.7 %copy-start = (bf16[1024,1024]{1,0:T(8,128)(2,1)S(1)}, bf16[1024,1024]{1,0:T(8,128)(2,1)}, u32[]{:S(2)}) copy-start(bf16[1024,1024]{1,0:T(8,128)(2,1)} %param.22) | copy-start | bytes 6291460
  7.2 43.0 %copy-start.3 = (bf16[128,1024]{1,0:T(8,128)(2,1)S(1)}, bf16[128,1024]{1,0:T(8,128)(2,1)}, u32[]{:S(2)}) copy-start(bf16[128,1024]{1,0:T(8,128)(2,1)} %param.17) | copy-start | bytes 786436
  7.2 43.4 %copy-start.8 = (f32[1024]{0:T(1024)S(1)}, f32[1024]{0:T(1024)}, u32[]{:S(2)}) copy-start(f32[1024]{0:T(1024)} %param.20) | copy-start | bytes 12292
  7.2 42.2 %all-gather.7.cloned.1.call-start = ((), (), s32[]{:S(2)}) async-start(), calls=%async_computation | async-start | bytes 4718592 | tf_op jit(solution)/shard_map/all_gather | solution.py:142
  7.9 341.7 %all-gather.9.cloned.1.call-start = ((), (), s32[]{:S(2)}) async-start(), calls=%async_computation.1 | async-start | bytes 20971520 | tf_op jit(solution)/shard_map/all_gather | solution.py:143
  49.4 336.4 %all-gather.11.cloned.1.call-start = ((), (), s32[]{:S(2)}) async-start(), calls=%async_computation.2 | async-start | bytes 4718592 | tf_op jit(solution)/shard_map/all_gather | solution.py:158
  50.1 374.1 %all-gather.13.cloned.1.call-start = ((), (), s32[]{:S(2)}) async-start(), calls=%async_computation.3 | async-start | bytes 4718592 | tf_op jit(solution)/shard_map/all_gather | solution.py:162
  55.2 12.0 %collective-permute-start.1 = (bf16[128,1024]{1,0:T(8,128)(2,1)S(1)}, bf16[128,1024]{1,0:T(8,128)(2,1)S(1)}, u32[]{:S(2)}, u32[]{:S(2)}) collective-permute-start(bf16[128,1024]{1,0:T(8,128)(2,1)S(1)} %get-tuple-element.318), channel_id=1, source_target_pairs={{0,1},{1,2},{2,3},{3,4},{4,5},{5,6},{6,7},{7,8},{8,9},{9,10},{10,1... | collective-permute-start | bytes 786440 | tf_op jit(solution)/shard_map/ppermute | solution.py:28
  58.6 19.2 %collective-permute-start = (bf16[128,1024]{1,0:T(8,128)(2,1)}, bf16[128,1024]{1,0:T(8,128)(2,1)}, u32[]{:S(2)}, u32[]{:S(2)}) collective-permute-start(bf16[128,1024]{1,0:T(8,128)(2,1)} %get-tuple-element.320), channel_id=1, source_target_pairs={{0,1},{1,2},{2,3},{3,4},{4,5},{5,6},{6,7},{7,8},{8,9},{9,10},{10,1... | collective-permute-start | bytes 786440 | tf_op jit(solution)/shard_map/ppermute | solution.py:28
  62.8 388.8 %all-gather.15.cloned.1.call-start = ((), (), s32[]{:S(2)}) async-start(), calls=%async_computation.4 | async-start | bytes 1179648 | tf_op jit(solution)/shard_map/all_gather | solution.py:17
  64.5 22.7 %copy-start.44 = (pred[128]{0:T(512)(128)(4,1)}, pred[128]{0:T(512)(128)(4,1)S(1)}, u32[]{:S(2)}) copy-start(pred[128]{0:T(512)(128)(4,1)S(1)} %subtract_compare_fusion.1) | copy-start | bytes 388
  83.7 20.1 %copy-start.12 = (f32[1,1024]{1,0:T(1,128)S(1)}, f32[1,1024]{1,0:T(1,128)}, u32[]{:S(2)}) copy-start(f32[1,1024]{1,0:T(1,128)} %get-tuple-element.323) | copy-start | bytes 12292
  83.7 20.1 %copy-start.13 = (f32[1,1024]{1,0:T(1,128)S(1)}, f32[1,1024]{1,0:T(1,128)}, u32[]{:S(2)}) copy-start(f32[1,1024]{1,0:T(1,128)} %get-tuple-element.324) | copy-start | bytes 12292
  83.7 20.1 %copy-start.14 = (f32[1,1024]{1,0:T(1,128)S(1)}, f32[1,1024]{1,0:T(1,128)}, u32[]{:S(2)}) copy-start(f32[1,1024]{1,0:T(1,128)} %get-tuple-element.325) | copy-start | bytes 12292
  83.7 20.1 %copy-start.15 = (f32[1,1024]{1,0:T(1,128)S(1)}, f32[1,1024]{1,0:T(1,128)}, u32[]{:S(2)}) copy-start(f32[1,1024]{1,0:T(1,128)} %get-tuple-element.326) | copy-start | bytes 12292
  83.7 20.1 %copy-start.16 = (f32[1,1024]{1,0:T(1,128)S(1)}, f32[1,1024]{1,0:T(1,128)}, u32[]{:S(2)}) copy-start(f32[1,1024]{1,0:T(1,128)} %get-tuple-element.327) | copy-start | bytes 12292
  83.7 20.1 %copy-start.17 = (f32[1,1024]{1,0:T(1,128)S(1)}, f32[1,1024]{1,0:T(1,128)}, u32[]{:S(2)}) copy-start(f32[1,1024]{1,0:T(1,128)} %get-tuple-element.328) | copy-start | bytes 12292
  83.7 20.1 %copy-start.18 = (f32[1,1024]{1,0:T(1,128)S(1)}, f32[1,1024]{1,0:T(1,128)}, u32[]{:S(2)}) copy-start(f32[1,1024]{1,0:T(1,128)} %get-tuple-element.329) | copy-start | bytes 12292
  83.7 20.1 %copy-start.19 = (f32[1,1024]{1,0:T(1,128)S(1)}, f32[1,1024]{1,0:T(1,128)}, u32[]{:S(2)}) copy-start(f32[1,1024]{1,0:T(1,128)} %get-tuple-element.330) | copy-start | bytes 12292
  83.8 20.1 %copy-start.20 = (f32[1,1024]{1,0:T(1,128)S(1)}, f32[1,1024]{1,0:T(1,128)}, u32[]{:S(2)}) copy-start(f32[1,1024]{1,0:T(1,128)} %get-tuple-element.331) | copy-start | bytes 12292
  83.8 20.1 %copy-start.21 = (f32[1,1024]{1,0:T(1,128)S(1)}, f32[1,1024]{1,0:T(1,128)}, u32[]{:S(2)}) copy-start(f32[1,1024]{1,0:T(1,128)} %get-tuple-element.332) | copy-start | bytes 12292
  83.8 20.1 %copy-start.22 = (f32[1,1024]{1,0:T(1,128)S(1)}, f32[1,1024]{1,0:T(1,128)}, u32[]{:S(2)}) copy-start(f32[1,1024]{1,0:T(1,128)} %get-tuple-element.333) | copy-start | bytes 12292
  83.8 20.1 %copy-start.23 = (f32[1,1024]{1,0:T(1,128)S(1)}, f32[1,1024]{1,0:T(1,128)}, u32[]{:S(2)}) copy-start(f32[1,1024]{1,0:T(1,128)} %get-tuple-element.334) | copy-start | bytes 12292
  83.8 20.1 %copy-start.24 = (f32[1,1024]{1,0:T(1,128)S(1)}, f32[1,1024]{1,0:T(1,128)}, u32[]{:S(2)}) copy-start(f32[1,1024]{1,0:T(1,128)} %get-tuple-element.335) | copy-start | bytes 12292
  83.8 20.1 %copy-start.25 = (f32[1,1024]{1,0:T(1,128)S(1)}, f32[1,1024]{1,0:T(1,128)}, u32[]{:S(2)}) copy-start(f32[1,1024]{1,0:T(1,128)} %get-tuple-element.336) | copy-start | bytes 12292
  83.8 20.1 %copy-start.26 = (f32[1,1024]{1,0:T(1,128)S(1)}, f32[1,1024]{1,0:T(1,128)}, u32[]{:S(2)}) copy-start(f32[1,1024]{1,0:T(1,128)} %get-tuple-element.337) | copy-start | bytes 12292
  83.8 20.1 %copy-start.27 = (f32[1,1024]{1,0:T(1,128)S(1)}, f32[1,1024]{1,0:T(1,128)}, u32[]{:S(2)}) copy-start(f32[1,1024]{1,0:T(1,128)} %get-tuple-element.338) | copy-start | bytes 12292
  83.8 20.1 %copy-start.28 = (f32[1,1024]{1,0:T(1,128)S(1)}, f32[1,1024]{1,0:T(1,128)}, u32[]{:S(2)}) copy-start(f32[1,1024]{1,0:T(1,128)} %get-tuple-element.339) | copy-start | bytes 12292
  87.3 16.4 %collective-permute-start.2 = (bf16[30,1024]{1,0:T(8,128)(2,1)S(1)}, bf16[30,1024]{1,0:T(8,128)(2,1)S(1)}, u32[]{:S(2)}, u32[]{:S(2)}) collective-permute-start(bf16[30,1024]{1,0:T(8,128)(2,1)S(1)} %slice.294), channel_id=1, source_target_pairs={{0,1},{1,2},{2,3},{3,4},{4,5},{5,6},{6,7},{7,8},{8,9},{9,10},{10,1... | collective-permute-start | bytes 184328 | tf_op jit(solution)/shard_map/ppermute | solution.py:28
  107.4 250.5 %copy-start.6 = (bf16[128,1024]{1,0:T(8,128)(2,1)}, bf16[128,1024]{1,0:T(8,128)(2,1)S(1)}, u32[]{:S(2)}) copy-start(bf16[128,1024]{1,0:T(8,128)(2,1)S(1)} %fusion.23) | copy-start | bytes 786436
  133.3 224.6 %copy-start.9 = (f32[8192]{0:T(1024)S(1)}, f32[8192]{0:T(1024)}, u32[]{:S(2)}) copy-start(f32[8192]{0:T(1024)} %param.28) | copy-start | bytes 98308
  427.9 186.2 %all-gather.17.cloned.1.call-start = ((), (), s32[]{:S(2)}) async-start(), calls=%async_computation.5 | async-start | bytes 37748736 | tf_op jit(solution)/shard_map/all_gather | solution.py:154
  (25 other events, 364.5 us)
Sparse Core Ops, SparseCore 0:
  9.9 39.4 all-gather.6
  50.9 298.6 all-gather.8
  351.5 34.1 all-gather.10
  387.5 36.7 all-gather.12
  428.0 23.4 all-gather.14
  453.2 160.7 all-gather.16
